TPU v7x, 32 devices: a whole 2x2x4 slice. The times are simulated.
32 devices in a mesh: subset: 4 (over x, core), slab: 8 (over z, y).
Axes of the slice: x: 2, y: 2, z: 4, core: 2. Of those that a mesh axis runs over, the one named last changes fastest.
Arguments:
- sinogram: bfloat16 [64, 64, 2048], P(('subset', 'slab')), may hold values from -12 to 12
- angles: float32 [64], P(('subset', 'slab')), may hold values from -3.140625 to 3.140625
- w_first: float32 [32, 27], replicated, may hold values from -1.25 to 1.25
- b_first: float32 [32], replicated, may hold values from -3 to 3
- w_second: float32 [32, 27], replicated, may hold values from -0.21875 to 0.21875
- b_second: float32 [1], replicated, may hold values from -3 to 3
Outputs:
- prediction: float32 [4, 32, 8, 1024], P('subset', 'slab')
- target_slab: float32 [4, 32, 8, 1024], P('subset', 'slab')
- loss: float32 [], replicated
- grad_w_first: float32 [32, 27], replicated
- grad_b_first: float32 [32], replicated
- grad_w_second: float32 [32, 27], replicated
- grad_b_second: float32 [1], replicated
All inputs are finite; a program needn't handle non-finite values.
Results may differ from a plain program's by a relative error of at most 0.00065.
The roundings to bfloat16 on the way count: a program that leaves them out, or rounds other values in their place, can miss the bound.
Values may be sent and summed in bfloat16 or wider, within the bound.
No kernel may reach another device: no remote copies, remote signals or barrier semaphores. Data moves between devices by JAX's collectives and lax.ppermute only.
A program may use at most 128 MiB of HBM per device.

v0:
```python
import functools
import math

import jax
import jax.numpy as jnp
from jax import lax
from jax.experimental import pallas as pl
from jax.experimental.pallas import tpu as pltpu
from jax.sharding import PartitionSpec as P


DET = 2048
X = 1024
Y = 8
LANES = 128
TAPS = 27
TILE = 256
BLOCK = 80
W_SECOND_AT = 32
B_SECOND_AT = 59
LOSS_AT = 64
GRAD_B_SECOND_AT = 65
HALO = 2
BOTH = ("subset", "slab")

RADIUS = math.hypot((X - 1) / 2.0, (Y - 1) / 2.0) + 0.25
FIRST_D = math.floor((DET - 1) / 2.0 - RADIUS)
LAST_D = math.floor((DET - 1) / 2.0 + RADIUS) + 1
D0 = FIRST_D - 8
DW = -(-(LAST_D + 1 - D0) // LANES) * LANES
READ_D = D0 // LANES * LANES
READ_W = -(-(D0 + DW - READ_D) // LANES) * LANES
assert D0 >= 0 and READ_D + READ_W <= DET

F32 = jnp.float32
BF16 = jnp.bfloat16
VMEM = pl.BlockSpec(memory_space=pltpu.VMEM)
SMEM = pl.BlockSpec(memory_space=pltpu.SMEM)


def vmem_mib(count):
    return pltpu.CompilerParams(vmem_limit_bytes=count * 2**20)


def iota(shape, dim):
    return lax.broadcasted_iota(jnp.int32, shape, dim)


def split2(value):
    high = value.astype(BF16)
    return high, (value - high.astype(F32)).astype(BF16)


def dot(a, b):
    return jnp.dot(a, b, preferred_element_type=F32)


def dot_nt(a, b):
    return lax.dot_general(a, b, (((1,), (1,)), ((), ())), preferred_element_type=F32)


def pack_kernel(depth, angle_ref, sino_ref, *refs):
    out_refs, (held_ref, rows_ref, cut_ref, sems) = refs[:-4], refs[-4:]
    views, z_count = sino_ref.shape[0], sino_ref.shape[1]
    n_slab = len(out_refs)
    rows = depth + 2 * HALO
    half = lax.axis_index("subset") % 2
    slab = lax.axis_index("slab")
    copies = [
        pltpu.make_async_copy(
            sino_ref.at[view, :, pl.ds(READ_D, READ_W)], held_ref.at[view], sems.at[view]
        )
        for view in range(views)
    ]
    for copy in copies:
        copy.start()
    lane = iota((rows, LANES), 1)
    zeros = jnp.zeros((8, DW), F32)
    rows_ref[0:8, :] = zeros
    rows_ref[8 + z_count : 16 + z_count, :] = zeros
    for view in range(views):
        angle = jnp.full((rows, LANES), angle_ref[view], F32)
        head = jnp.zeros((rows, LANES), F32)
        for which, left in enumerate((jnp.cos(angle), jnp.sin(angle))):
            for part in range(3):
                piece = left.astype(BF16).astype(F32)
                left = left - piece
                head = jnp.where(lane == 3 * which + part, piece, head)
        copies[view].wait()
        moved = pltpu.roll(held_ref[view].astype(F32), (READ_D - D0) % READ_W, 1)
        rows_ref[8 : 8 + z_count, :] = moved[:, 0:DW]
        for to in range(2 * n_slab):
            start = 8 + to * depth - HALO
            cut_ref[to] = rows_ref[start : start + rows, :]
            first = rows_ref[start : start + rows, 0:LANES]
            cut_ref[to, :, 0:LANES] = jnp.where(lane < 6, head, first)
        for apart, out_ref in enumerate(out_refs):
            to = jnp.bitwise_xor(slab, apart)
            mine = cut_ref[half * n_slab + to]
            other = cut_ref[(1 - half) * n_slab + to]
            out_ref[view] = jnp.concatenate([mine, other], axis=0).astype(BF16)


def pack(angles, sino, n_slab, depth):
    views, z_count = sino.shape[0], sino.shape[1]
    rows = depth + 2 * HALO
    return pl.pallas_call(
        functools.partial(pack_kernel, depth),
        out_shape=(jax.ShapeDtypeStruct((views, 2 * rows, DW), BF16),) * n_slab,
        in_specs=[SMEM, pl.BlockSpec(memory_space=pltpu.HBM)],
        out_specs=(VMEM,) * n_slab,
        scratch_shapes=[
            pltpu.VMEM((views, z_count, READ_W), BF16),
            pltpu.VMEM((z_count + 16, DW), F32),
            pltpu.VMEM((2 * n_slab, rows, DW), F32),
            pltpu.SemaphoreType.DMA((views,)),
        ],
        compiler_params=vmem_mib(8),
        name="pack",
    )(
        pltpu.with_memory_space_constraint(angles, pltpu.HBM),
        pltpu.with_memory_space_constraint(sino, pltpu.HBM),
    )


def project_kernel(count, scale, *refs):
    data_refs = refs[:count]
    init_refs = refs[count:-9]
    mine_ref, other_ref, own_ref, away_ref, low_ref, high_ref, tab_ref, scal_ref, sem = refs[-9:]
    each = data_refs[0].shape[0]
    views, rows = count * each, data_refs[0].shape[1]
    window = rows // 2
    centre = (DET - 1) / 2.0
    for place, data_ref in enumerate(data_refs):
        values = data_ref[...].astype(F32)
        moved = pltpu.roll(values.reshape(each * rows, DW), DW - 1, 1).reshape(values.shape)
        here = slice(place * each, (place + 1) * each)
        for tile in range(DW // LANES):
            cols = slice(tile * LANES, (tile + 1) * LANES)
            low_ref[here, tile] = values[:, :, cols]
            high_ref[here, tile] = moved[:, :, cols]
    head = low_ref[:, 0, 0, :]
    cosine = jnp.broadcast_to(head[:, 0:1] + head[:, 1:2] + head[:, 2:3], (views, LANES))
    sine = jnp.broadcast_to(head[:, 3:4] + head[:, 4:5] + head[:, 5:6], (views, LANES))

    def at(col, row):
        return col * cosine + row * sine + centre

    start = (iota((views, LANES), 1) % (X // LANES)).astype(F32) * LANES - (X - 1) / 2.0
    stop = start + (LANES - 1.0)
    edge = (Y - 1) / 2.0
    least = jnp.minimum(
        jnp.minimum(at(start, -edge), at(stop, -edge)), jnp.minimum(at(start, edge), at(stop, edge))
    )
    tab_ref[0] = cosine
    tab_ref[1] = sine
    tab_ref[2] = ((jnp.floor(least).astype(jnp.int32) - D0) // LANES).astype(F32)
    copy = pltpu.make_async_copy(tab_ref, scal_ref, sem)
    copy.start()
    copy.wait()

    lane = iota((views, LANES), 1)
    row_of_lane = (lane // (X // LANES) % Y).astype(F32) - edge
    ends = jnp.floor(at(stop, row_of_lane)) - jnp.floor(at(start, row_of_lane))
    apart = jnp.max(jnp.abs(ends)) >= float(LANES)

    lanes = iota((Y, LANES), 1)
    column = lanes.astype(F32)
    row_pos = iota((Y, LANES), 0).astype(F32) - edge

    def all_blocks(distinct):
        def one_block(block, carry):
            left = block.astype(F32) * LANES - (X - 1) / 2.0
            col = column + left

            def one_view(view, sums):
                tile = scal_ref[2, view, block].astype(jnp.int32)
                cos_part = scal_ref[0, view, 0]
                sin_part = row_pos * scal_ref[1, view, 0]
                position = col * cos_part + sin_part + centre
                lower = jnp.floor(position)
                weight_low = jnp.maximum(0.0, 1.0 - jnp.abs(position - lower))
                weight_high = jnp.maximum(0.0, 1.0 - jnp.abs(position - (lower + 1.0)))
                weight_low = weight_low.astype(BF16).astype(F32)
                weight_high = weight_high.astype(BF16).astype(F32)
                base = D0 + tile * LANES
                index = lower.astype(jnp.int32) - base
                second = index >= LANES
                index = jnp.bitwise_and(index, LANES - 1)
                if distinct:
                    end1 = left * cos_part + sin_part + centre
                    end2 = (left + (LANES - 1.0)) * cos_part + sin_part + centre
                    least_index = jnp.floor(jnp.minimum(end1, end2)).astype(jnp.int32) - base
                    in_first = lanes >= least_index

                def take(ref, z):
                    def line(at_tile):
                        return ref[view, at_tile, pl.ds(z, Y, stride=0), :]

                    def pick(values):
                        return jnp.take_along_axis(
                            values, index, axis=1, mode="promise_in_bounds"
                        )

                    one, two = line(tile), line(tile + 1)
                    if distinct:
                        return pick(jnp.where(in_first, one, two))
                    return jnp.where(second, pick(two), pick(one))

                return tuple(
                    sums[z] + (weight_low * take(low_ref, z) + weight_high * take(high_ref, z))
                    for z in range(rows)
                )

            cols = pl.ds(pl.multiple_of(block * LANES, LANES), LANES)
            if init_refs:
                sums = tuple(
                    init_refs[z // window][z % window, :, cols] for z in range(rows)
                )
            else:
                sums = tuple(jnp.zeros((Y, LANES), F32) for _ in range(rows))
            sums = lax.fori_loop(0, views, one_view, sums, unroll=views if distinct else 1)
            for z in range(rows):
                done = sums[z] * scale if scale else sums[z]
                at_z = z % window
                (mine_ref, other_ref)[z // window][at_z, :, cols] = done
                if scale and HALO <= at_z < window - HALO:
                    (own_ref, away_ref)[z // window][at_z - HALO, :, cols] = done
            return carry

        lax.fori_loop(0, X // LANES, one_block, 0)

    pl.when(apart)(lambda: all_blocks(False))
    pl.when(jnp.logical_not(apart))(lambda: all_blocks(True))


def project(chunks, init, scale):
    count = len(chunks)
    views, rows = count * chunks[0].shape[0], chunks[0].shape[1]
    whole = jax.ShapeDtypeStruct((rows // 2, Y, X), F32)
    inner = jax.ShapeDtypeStruct((rows // 2 - 2 * HALO if scale else 1, Y, X), F32)
    return pl.pallas_call(
        functools.partial(project_kernel, count, scale),
        out_shape=(whole, whole, inner, inner),
        in_specs=[VMEM] * (count + len(init)),
        out_specs=(VMEM,) * 4,
        scratch_shapes=[
            pltpu.VMEM((views, DW // LANES, rows, LANES), F32),
            pltpu.VMEM((views, DW // LANES, rows, LANES), F32),
            pltpu.VMEM((3, views, LANES), F32),
            pltpu.SMEM((3, views, LANES), F32),
            pltpu.SemaphoreType.DMA,
        ],
        compiler_params=vmem_mib(14),
        cost_estimate=pl.CostEstimate(
            flops=4_000_000_000, bytes_accessed=1_500_000, transcendentals=0
        ),
        name="project",
    )(*chunks, *init)


def first_column(dx, dz, dy):
    return 9 * dz + 3 * dy + dx


def second_column(dx, dz, dy):
    return W_SECOND_AT + (TAPS - 1) - first_column(dx, dz, dy)


def spread(params, column_of, bias):
    channels = params.shape[0]
    height = channels * Y
    high, low = split2(params)
    both = jnp.concatenate([high, low], axis=1)
    rep = (iota((height, channels), 0) // Y == iota((height, channels), 1)).astype(F32)
    rep = rep.astype(BF16)
    shape = (2 * LANES, TILE)
    source = iota(shape, 0)
    col = iota(shape, 1)
    part, inner = col // BLOCK, col % BLOCK
    wanted_half = jnp.where(part == 2, 1, 0)
    usable = (part < 3) & (source // LANES == wanted_half)
    out_col = iota((height, TILE), 1)
    out_inner = out_col % BLOCK
    out_y = iota((height, TILE), 0) % Y
    total = jnp.zeros((height, TILE), F32)
    for dy in range(3):
        wanted = column_of(inner // 24, (inner // 8) % 3, dy)
        pick = usable & (inner < 72) & (source % LANES == wanted)
        if bias and dy == 1:
            pick = pick | (usable & (inner == 72) & (source % LANES == TAPS))
        chosen = dot(both, pick.astype(F32).astype(BF16)).astype(BF16)
        here = (out_inner < 72) & (out_inner % 8 - out_y + 1 == dy)
        if bias and dy == 1:
            here = here | (out_inner == 72)
        total = total + jnp.where(here, dot(rep, chosen), 0.0)
    return total.astype(BF16)


def gather_taps(grads, channels):
    height = channels * Y
    col = iota((height, LANES), 1)
    row_y = iota((height, LANES), 0) % Y
    inner = iota((LANES, LANES), 0)
    to = iota((LANES, LANES), 1)
    pieces = []
    picks = []
    for grad, column_of, bias in grads:
        for dy in range(3):
            here = (col < 72) & (col % 8 - row_y + 1 == dy)
            pick = (inner < 72) & (to == column_of(inner // 24, (inner // 8) % 3, dy))
            if bias and dy == 1:
                here = here | (col == 72)
                pick = pick | ((inner == 72) & (to == TAPS))
            masked = jnp.where(here, grad, 0.0).reshape(channels, Y, LANES)
            pieces.append(jnp.sum(masked, axis=1))
            picks.append(pick.astype(F32))
    return jnp.dot(
        jnp.concatenate(pieces, axis=1),
        jnp.concatenate(picks, axis=0),
        precision=lax.Precision.HIGHEST,
        preferred_element_type=F32,
    )


def shift_columns(value, by):
    if by == 0:
        return value
    rolled = pltpu.roll(value, (-by) % X, 1)
    lane = iota(value.shape, 1)
    return jnp.where(lane == (X - 1 if by > 0 else 0), 0.0, rolled)


def fill_shifted(ref, field):
    for dx in range(3):
        ref[dx] = shift_columns(field, dx - 1)


def patch(ref, slice_index, tile):
    at = pl.multiple_of(slice_index * Y, Y)
    cols = slice(tile * TILE, (tile + 1) * TILE)
    pieces = [ref[dx, pl.ds(at, 3 * Y), cols] for dx in range(3)]
    pieces.append((iota((8, TILE), 0) == 0).astype(F32))
    high, low = split2(jnp.concatenate(pieces, axis=0))
    return high, low


def apply_spread(weights, high, low):
    return dot(weights[:, 0 : 3 * BLOCK], jnp.concatenate([high, low, high], axis=0))


def slice_flag(hidden_slice, hidden_count):
    n_slab = lax.axis_size("slab")
    place = (lax.axis_index("subset") % 2) * n_slab + lax.axis_index("slab")
    outside = ((hidden_slice == 0) & (place == 0)) | (
        (hidden_slice == hidden_count - 1) & (place == 2 * n_slab - 1)
    )
    return jnp.where(outside, 0.0, 1.0).astype(F32)


def weights_kernel(params_ref, first_ref, second_ref, turned_ref):
    params = params_ref[...]
    second = spread(params, second_column, False)
    first_ref[...] = spread(params, first_column, True)
    second_ref[...] = second
    turned_ref[...] = second.astype(F32).T.astype(BF16)


def weights(params):
    height = params.shape[0] * Y
    return pl.pallas_call(
        weights_kernel,
        out_shape=(
            jax.ShapeDtypeStruct((height, TILE), BF16),
            jax.ShapeDtypeStruct((height, TILE), BF16),
            jax.ShapeDtypeStruct((TILE, height), BF16),
        ),
        in_specs=[VMEM],
        out_specs=(VMEM,) * 3,
        compiler_params=vmem_mib(8),
        name="weights",
    )(params)


def forward_kernel(
    mine_ref,
    came_ref,
    params_ref,
    first_ref,
    turned_ref,
    pred_ref,
    again_ref,
    shifted_ref,
    hidden_ref,
    acc_ref,
):
    rows = mine_ref.shape[0]
    hidden_count = rows - 2
    height = first_ref.shape[0]
    first = first_ref[...]
    fill_shifted(shifted_ref, (mine_ref[...] + came_ref[...]).reshape(rows * Y, X))
    acc_ref[...] = jnp.zeros(acc_ref.shape, F32)

    def one_slice(hidden_slice, carry):
        flag = slice_flag(hidden_slice, hidden_count)
        at = pl.multiple_of(hidden_slice * Y, Y)
        kept = pl.ds(pl.multiple_of(hidden_slice * height, height), height)
        for tile in range(X // TILE):
            cols = slice(tile * TILE, (tile + 1) * TILE)
            high, low = patch(shifted_ref, hidden_slice, tile)
            hidden = jnp.maximum(apply_spread(first, high, low), 0.0) * flag
            h_high, h_low = split2(hidden)
            hidden_ref[kept, cols] = h_high
            main = dot(turned_ref[BLOCK : 3 * BLOCK], h_high)
            taps = main[0:BLOCK] + main[BLOCK : 2 * BLOCK] + dot(turned_ref[0:BLOCK], h_low)
            for dx in range(3):
                acc_ref[dx, pl.ds(at, 3 * Y), cols] += taps[24 * dx : 24 * dx + 24]
        return carry

    lax.fori_loop(0, hidden_count, one_slice, 0)
    inner = slice(HALO * Y, (rows - HALO) * Y)
    added = acc_ref[1, inner, :]
    for dx in (0, 2):
        added = added + shift_columns(acc_ref[dx, inner, :], 1 - dx)
    own = shifted_ref[1, inner, :]
    bias = params_ref[0:1, B_SECOND_AT : B_SECOND_AT + 1]
    pred = (own + added + bias).reshape(pred_ref.shape)
    pred_ref[...] = pred
    again_ref[...] = pred


def forward(mine, came, params, first, turned):
    rows = mine.shape[0]
    height = first.shape[0]
    own = jax.ShapeDtypeStruct((rows - 2 * HALO, Y, X), F32)
    return pl.pallas_call(
        forward_kernel,
        out_shape=(
            own,
            own,
            jax.ShapeDtypeStruct((3, rows * Y, X), F32),
            jax.ShapeDtypeStruct(((rows - 2) * height, X), BF16),
        ),
        in_specs=[VMEM] * 5,
        out_specs=(VMEM,) * 4,
        scratch_shapes=[pltpu.VMEM((3, rows * Y, X), F32)],
        cost_estimate=pl.CostEstimate(
            flops=20_000_000_000, bytes_accessed=2_000_000, transcendentals=0
        ),
        compiler_params=vmem_mib(18),
        name="forward",
    )(mine, came, params, first, turned)


def padded_rows(high, low):
    none = jnp.zeros((LANES - BLOCK, high.shape[1]), BF16)
    return jnp.concatenate([high, none, low, none], axis=0)


def backward_kernel(cells, others, shifted_ref, hidden_ref, pred_ref, second_ref, *refs):
    part_refs = refs[: 2 * others]
    out_ref, target_out_ref, grad_ref, acc1_ref, acc2_ref = refs[2 * others :]
    rows = shifted_ref.shape[1] // Y
    hidden_count = rows - 2
    height = second_ref.shape[0]
    channels = height // Y
    target = part_refs[0][...]
    for part_ref in part_refs[1:]:
        target = target + part_ref[...]
    target = target if others == 1 else target / others
    target_out_ref[...] = target
    diff = (pred_ref[...] - target).reshape((rows - 2 * HALO) * Y, X)
    resid = 2.0 * diff / cells
    loss = jnp.sum(diff * diff, keepdims=True) / cells
    grad_b2 = jnp.sum(resid, keepdims=True)
    inner = slice(HALO * Y, (rows - HALO) * Y)
    for dx in range(3):
        grad_ref[dx, 0 : HALO * Y, :] = jnp.zeros((HALO * Y, X), F32)
        grad_ref[dx, (rows - HALO) * Y : rows * Y, :] = jnp.zeros((HALO * Y, X), F32)
        grad_ref[dx, inner, :] = shift_columns(resid, dx - 1)
    acc1_ref[...] = jnp.zeros(acc1_ref.shape, F32)
    acc2_ref[...] = jnp.zeros(acc2_ref.shape, F32)
    second = second_ref[...]

    def one_slice(hidden_slice, carry):
        kept = pl.ds(pl.multiple_of(hidden_slice * height, height), height)
        sum1 = None
        sum2 = None
        for tile in range(X // TILE):
            cols = slice(tile * TILE, (tile + 1) * TILE)
            high, low = patch(shifted_ref, hidden_slice, tile)
            g_high, g_low = patch(grad_ref, hidden_slice, tile)
            hidden = hidden_ref[kept, cols]
            grad_hidden = apply_spread(second, g_high, g_low)
            grad_pre = jnp.where(hidden.astype(F32) > 0.0, grad_hidden, 0.0).astype(BF16)
            part1 = dot_nt(grad_pre, padded_rows(high, low))
            part2 = dot_nt(hidden, padded_rows(g_high, g_low))
            sum1 = part1 if sum1 is None else sum1 + part1
            sum2 = part2 if sum2 is None else sum2 + part2
        acc1_ref[...] += sum1
        acc2_ref[...] += sum2
        return carry

    lax.fori_loop(0, hidden_count, one_slice, 0)

    def folded(ref):
        return ref[:, 0:LANES] + ref[:, LANES : 2 * LANES]

    total = gather_taps(
        ((folded(acc1_ref), first_column, True), (folded(acc2_ref), second_column, False)), channels
    )
    lane = iota((channels, LANES), 1)
    diagonal = lane == iota((channels, LANES), 0)
    line = jnp.sum(jnp.where(diagonal, total[:, TAPS : TAPS + 1], 0.0), axis=0, keepdims=True)
    line = jnp.where(lane[0:8] == LOSS_AT, loss, jnp.broadcast_to(line, (8, LANES)))
    out_ref[0:channels, :] = total
    out_ref[channels : channels + 8, :] = jnp.where(lane[0:8] == GRAD_B_SECOND_AT, grad_b2, line)


def backward(shifted, hidden, pred, parts, second, cells):
    height = second.shape[0]
    return pl.pallas_call(
        functools.partial(backward_kernel, cells, len(parts) // 2),
        out_shape=(
            jax.ShapeDtypeStruct((height // Y + 8, LANES), F32),
            jax.ShapeDtypeStruct(pred.shape, F32),
        ),
        in_specs=[VMEM] * (4 + len(parts)),
        out_specs=(VMEM, VMEM),
        scratch_shapes=[
            pltpu.VMEM(shifted.shape, F32),
            pltpu.VMEM((height, 2 * LANES), F32),
            pltpu.VMEM((height, 2 * LANES), F32),
        ],
        compiler_params=vmem_mib(18),
        name="backward",
    )(shifted, hidden, pred, second, *parts)


def finish_kernel(one_ref, two_ref, loss_ref, w1_ref, b1_ref, w2_ref, b2_ref):
    total = one_ref[...] + two_ref[...]
    channels = w1_ref.shape[0]
    line = total[channels : channels + 1]
    loss_ref[...] = line[:, LOSS_AT : LOSS_AT + 1]
    w1_ref[...] = total[0:channels, 0:TAPS]
    b1_ref[...] = line[:, 0:channels]
    w2_ref[...] = total[0:channels, W_SECOND_AT : W_SECOND_AT + TAPS]
    b2_ref[...] = line[:, GRAD_B_SECOND_AT : GRAD_B_SECOND_AT + 1]


def sum_everywhere(value, channels):
    devices = lax.axis_size("subset") * lax.axis_size("slab")
    apart = 1
    while True:
        arrived = lax.ppermute(value, BOTH, [(i, i ^ apart) for i in range(devices)])
        apart *= 2
        if apart == devices:
            break
        value = value + arrived
    shapes = ((1, 1), (channels, TAPS), (1, channels), (channels, TAPS), (1, 1))
    return pl.pallas_call(
        finish_kernel,
        out_shape=tuple(jax.ShapeDtypeStruct(shape, F32) for shape in shapes),
        in_specs=[VMEM, VMEM],
        out_specs=(VMEM,) * 5,
        compiler_params=vmem_mib(1),
        name="finish",
    )(value, arrived)


def body(sinogram, angles, w_first, b_first, w_second, b_second):
    n_sub = lax.axis_size("subset") // 2
    n_slab = lax.axis_size("slab")
    devices = 2 * n_sub * n_slab
    group = 2 * n_slab
    local_views, z_count = sinogram.shape[0], sinogram.shape[1]
    depth = z_count // group
    channels = w_first.shape[0]
    scale = math.pi / (local_views * group)
    cells = float(n_sub * z_count * Y * X)
    assert devices & (devices - 1) == 0 and n_slab > 1 and channels == 32 and depth >= HALO

    sent = pack(angles, sinogram, n_slab, depth)

    def exchange(value, distance):
        return lax.ppermute(value, BOTH, [(i, i ^ distance) for i in range(devices)])

    arrived = [sent[0]] + [None] * (n_slab - 1)
    for distance in range(1, n_slab):
        arrived[distance] = exchange(sent[distance], distance)
    near = n_slab // 2
    sums = project(arrived[:near], (), 0.0)
    sums, w_first, b_first, w_second, b_second = lax.optimization_barrier(
        (sums, w_first, b_first, w_second, b_second)
    )
    params = jnp.concatenate(
        [
            w_first,
            b_first[:, None],
            jnp.zeros((channels, W_SECOND_AT - TAPS - 1), F32),
            w_second,
            jnp.broadcast_to(b_second, (channels, LANES - W_SECOND_AT - TAPS)),
        ],
        axis=1,
    )
    sums, (first, second, turned) = lax.optimization_barrier((sums, weights(params)))
    mine, other, own, away = project(arrived[near:], sums[:2], scale)
    came = exchange(other, n_slab)
    parts = []
    for apart in range(1, n_sub):
        straight = [(i, (i + apart * group) % devices) for i in range(devices)]
        crossed = [(i, j ^ n_slab) for i, j in straight]
        parts.append(lax.ppermute(own, BOTH, straight))
        parts.append(lax.ppermute(away, BOTH, crossed))

    pred, again, shifted, hidden = forward(mine, came, params, first, turned)
    partial, target = backward(shifted, hidden, again, parts, second, cells)
    loss, grad_w1, grad_b1, grad_w2, grad_b2 = sum_everywhere(partial, channels)
    return (
        pred[None],
        target[None],
        loss.reshape(()),
        grad_w1,
        grad_b1.reshape(-1),
        grad_w2,
        grad_b2.reshape(-1),
    )


def solution(mesh):
    return jax.shard_map(
        body,
        mesh=mesh,
        in_specs=(P(BOTH, None, None), P(BOTH), P(), P(), P(), P()),
        out_specs=(
            P("subset", "slab", None, None),
            P("subset", "slab", None, None),
            P(),
            P(),
            P(),
            P(),
            P(),
        ),
        check_vma=False,
    )
```

profile of v0, /device:TPU:0, one launch (start us, length us, event | category | flops | bytes accessed | tf_op | source)
XLA Modules:
  0.0 58.9 jit_solution(9386668691642763748)
XLA Ops:
  0.6 2.0 %pack.1 = (bf16[2,16,1152]{2,1,0:T(8,128)(2,1)S(1)}, bf16[2,16,1152]{2,1,0:T(8,128)(2,1)S(1)}, bf16[2,16,1152]{2,1,0:T(8,128)(2,1)S(1)}, bf16[2,16,1152]{2,1,0:T...) custom-call(f32[2]{0:T(128)} %angle_ref.1, ...), custom_call_target="tpu_custom_call" | custom-call | tf_op jit(solution)/shard_map/pack/pallas_call | solution.py:107
  2.7 3.1 %collective-permute-start.4 = (bf16[2,16,1152]{2,1,0:T(8,128)(2,1)S(1)}, bf16[2,16,1152]{2,1,0:T(8,128)(2,1)S(1)}, u32[]{:S(2)}, u32[]{:S(2)}) collective-permute-start(bf16[2,16,1152]{2,1,0:T(8,128)(2,1)S(1)} %get-tuple-element.51), channel_id=1, source_target_pairs={{0,1},{1,0},{2,3},{3,2},{4,5},{5,4},{6,7},{7,6},{8,9},{9,8},{10,11... | collective-permute-start | bytes 221192 | tf_op jit(solution)/shard_map/ppermute | solution.py:586
  5.7 1.6 %collective-permute-start.5 = (bf16[2,16,1152]{2,1,0:T(8,128)(2,1)S(1)}, bf16[2,16,1152]{2,1,0:T(8,128)(2,1)S(1)}, u32[]{:S(2)}, u32[]{:S(2)}) collective-permute-start(bf16[2,16,1152]{2,1,0:T(8,128)(2,1)S(1)} %get-tuple-element.52), channel_id=1, source_target_pairs={{0,2},{1,3},{2,0},{3,1},{4,6},{5,7},{6,4},{7,5},{8,10},{9,11},{10,... | collective-permute-start | bytes 221192 | tf_op jit(solution)/shard_map/ppermute | solution.py:586
  7.3 0.0 collective-permute-start.6
  7.3 3.0 %collective-permute-start = (bf16[2,16,1152]{2,1,0:T(8,128)(2,1)S(1)}, bf16[2,16,1152]{2,1,0:T(8,128)(2,1)S(1)}, u32[]{:S(2)}, u32[]{:S(2)}) collective-permute-start(bf16[2,16,1152]{2,1,0:T(8,128)(2,1)S(1)} %get-tuple-element.46), channel_id=1, source_target_pairs={{0,4},{1,5},{2,6},{3,7},{4,0},{5,1},{6,2},{7,3},{8,12},{9,13},{10,... | collective-permute-start | bytes 221192 | tf_op jit(solution)/shard_map/ppermute | solution.py:586
  10.3 1.3 %collective-permute-start.1 = (bf16[2,16,1152]{2,1,0:T(8,128)(2,1)S(1)}, bf16[2,16,1152]{2,1,0:T(8,128)(2,1)S(1)}, u32[]{:S(2)}, u32[]{:S(2)}) collective-permute-start(bf16[2,16,1152]{2,1,0:T(8,128)(2,1)S(1)} %get-tuple-element.47), channel_id=1, source_target_pairs={{0,5},{1,4},{2,7},{3,6},{4,1},{5,0},{6,3},{7,2},{8,13},{9,12},{10,... | collective-permute-start | bytes 221192 | tf_op jit(solution)/shard_map/ppermute | solution.py:586
  12.2 0.0 collective-permute-done.4.refs_1_
  12.2 3.7 %collective-permute-start.2 = (bf16[2,16,1152]{2,1,0:T(8,128)(2,1)S(1)}, bf16[2,16,1152]{2,1,0:T(8,128)(2,1)S(1)}, u32[]{:S(2)}, u32[]{:S(2)}) collective-permute-start(bf16[2,16,1152]{2,1,0:T(8,128)(2,1)S(1)} %get-tuple-element.48), channel_id=1, source_target_pairs={{0,6},{1,7},{2,4},{3,5},{4,2},{5,3},{6,0},{7,1},{8,14},{9,15},{10,... | collective-permute-start | bytes 221192 | tf_op jit(solution)/shard_map/ppermute | solution.py:586
  15.9 0.0 collective-permute-done.5.refs_2_
  15.9 0.0 collective-permute-start.3
  15.9 0.0 collective-permute-done.6.refs_3_
  15.9 0.0 copy-start.2
  15.9 0.0 copy-start
  15.9 0.0 copy-start.1
  16.0 4.8 %project.2 = (f32[8,8,1024]{2,1,0:T(8,128)S(1)}, f32[8,8,1024]{2,1,0:T(8,128)S(1)}, f32[1,8,1024]{2,1,0:T(8,128)}, f32[1,8,1024]{2,1,0:T(8,128)}) custom-call(bf16[2,16,1152]{2,1,0:T(8,128)(2,1)S(1)} %get-tuple-element.50.refs_0_, bf16[2,16,1152]{2,1,0:T(8,128)(2,1)S(1)} %collective-permute-done.4.refs_1_, ...), custom_call_target="tpu_custom_call" | custom-call | flops 4000000000 | bytes 1500000 | tf_op jit(solution)/shard_map/project/pallas_call | solution.py:242
  20.8 0.0 copy-done.2
  20.8 0.1 copy.13
  20.9 0.0 copy-done
  20.9 0.0 copy-done.1
  20.9 0.1 concatenate.3.params_ref
  21.0 0.9 %weights.1 = (bf16[256,256]{1,0:T(8,128)(2,1)S(1)}, bf16[256,256]{1,0:T(8,128)(2,1)S(1)}, bf16[256,256]{1,0:T(8,128)(2,1)S(1)}) custom-call(f32[32,128]{1,0:T(8,128)S(1)} %concatenate.3.params_ref), custom_call_target="tpu_custom_call" | custom-call | tf_op jit(solution)/shard_map/weights/pallas_call | solution.py:371
  21.9 0.0 collective-permute-done.refs_0_
  21.9 0.0 collective-permute-done.1.refs_1_
  21.9 0.0 collective-permute-done.2.refs_2_
  21.9 1.1 %collective-permute-done.3.refs_3_ = bf16[2,16,1152]{2,1,0:T(8,128)(2,1)S(1)} collective-permute-done((bf16[2,16,1152]{2,1,0:T(8,128)(2,1)S(1)}, bf16[2,16,1152]{2,1,0:T(8,128)(2,1)S(1)}, u32[]{:S(2)}, u32[]{:S(2)}) %collective-permute-start.3) | collective-permute-done | bytes 73760 | tf_op jit(solution)/shard_map/ppermute | solution.py:586
  23.1 4.2 %project.3 = (f32[8,8,1024]{2,1,0:T(8,128)S(1)}, f32[8,8,1024]{2,1,0:T(8,128)S(1)}, f32[4,8,1024]{2,1,0:T(8,128)S(1)}, f32[4,8,1024]{2,1,0:T(8,128)S(1)}) custom-call(bf16[2,16,1152]{2,1,0:T(8,128)(2,1)S(1)} %collective-permute-done.refs_0_, bf16[2,16,1152]{2,1,0:T(8,128)(2,1)S(1)} %collective-permute-done.1.refs_1_, ...), custom_call_target="tpu_custom_call" | custom-call | flops 4000000000 | bytes 1500000 | tf_op jit(solution)/shard_map/project/pallas_call | solution.py:242
  27.2 0.1 collective-permute-start.7
  27.3 1.6 %collective-permute-start.8 = (f32[4,8,1024]{2,1,0:T(8,128)S(1)}, f32[4,8,1024]{2,1,0:T(8,128)S(1)}, u32[]{:S(2)}, u32[]{:S(2)}) collective-permute-start(f32[4,8,1024]{2,1,0:T(8,128)S(1)} %get-tuple-element.76), channel_id=1, source_target_pairs={{0,16},{1,17},{2,18},{3,19},{4,20},{5,21},{6,22},{7,23},{8,24},{9,... | collective-permute-start | bytes 393224 | tf_op jit(solution)/shard_map/ppermute | solution.py:613
  28.9 0.3 collective-permute-start.9
  29.2 0.0 collective-permute-done.7.came_ref
  29.2 4.8 %forward.1 = (f32[4,8,1024]{2,1,0:T(8,128)}, f32[4,8,1024]{2,1,0:T(8,128)S(1)}, f32[3,64,1024]{2,1,0:T(8,128)S(1)}, bf16[1536,1024]{1,0:T(8,128)(2,1)S(1)}) custom-call(f32[8,8,1024]{2,1,0:T(8,128)S(1)} %get-tuple-element.67.mine_ref, f32[8,8,1024]{2,1,0:T(8,128)S(1)} %collective-permute-done.7.came_ref, f32[32,128]{1,0:T(8,128)S(1)} %concatenate.3.params_ref, ...), custom_call_target="tpu_custom_call" | custom-call | flops 20000000000 | bytes 2000000 | tf_op jit(solution)/shard_map/forward/pallas_call | solution.py:436
  34.0 0.0 collective-permute-done.8.refs_0_
  34.0 1.5 %collective-permute-done.9.refs_1_ = f32[4,8,1024]{2,1,0:T(8,128)S(1)} collective-permute-done((f32[4,8,1024]{2,1,0:T(8,128)S(1)}, f32[4,8,1024]{2,1,0:T(8,128)S(1)}, u32[]{:S(2)}, u32[]{:S(2)}) %collective-permute-start.9) | collective-permute-done | bytes 131104 | tf_op jit(solution)/shard_map/ppermute | solution.py:614
  35.5 5.0 %backward.1 = (f32[40,128]{1,0:T(8,128)S(1)}, f32[4,8,1024]{2,1,0:T(8,128)}) custom-call(f32[3,64,1024]{2,1,0:T(8,128)S(1)} %get-tuple-element.72.shifted_ref, bf16[1536,1024]{1,0:T(8,128)(2,1)S(1)} %get-tuple-element.73.hidden_ref, f32[4,8,1024]{2,1,0:T(8,128)S(1)} %get-tuple-element.74.pred_ref, bf16[256,256]{1,0:T(8,128)(2,1)S(1)} %get-tuple-element.75.second_ref, ...), custom_call_target="tpu_custom_call" | custom-call | tf_op jit(solution)/shard_map/backward/pallas_call | solution.py:522
  40.5 0.6 %collective-permute-start.10 = (f32[40,128]{1,0:T(8,128)S(1)}, f32[40,128]{1,0:T(8,128)S(1)}, u32[]{:S(2)}, u32[]{:S(2)}) collective-permute-start(f32[40,128]{1,0:T(8,128)S(1)} %get-tuple-element.79), channel_id=1, source_target_pairs={{0,1},{1,0},{2,3},{3,2},{4,5},{5,4},{6,7},{7,6},{8,9},{9,8},{10,11... | collective-permute-start | bytes 61448 | tf_op jit(solution)/shard_map/ppermute | solution.py:555
  41.1 3.2 %collective-permute-done.10 = f32[40,128]{1,0:T(8,128)S(1)} collective-permute-done((f32[40,128]{1,0:T(8,128)S(1)}, f32[40,128]{1,0:T(8,128)S(1)}, u32[]{:S(2)}, u32[]{:S(2)}) %collective-permute-start.10) | collective-permute-done | bytes 20512 | tf_op jit(solution)/shard_map/ppermute | solution.py:555
  44.4 2.2 %collective-permute-start.11 = (f32[40,128]{1,0:T(8,128)S(1)}, f32[40,128]{1,0:T(8,128)S(1)}, u32[]{:S(2)}, u32[]{:S(2)}) collective-permute-start(f32[40,128]{1,0:T(8,128)S(1)} %add.12), channel_id=1, source_target_pairs={{0,2},{1,3},{2,0},{3,1},{4,6},{5,7},{6,4},{7,5},{8,10},{9,11},{10,... | collective-permute-start | bytes 61448 | tf_op jit(solution)/shard_map/ppermute | solution.py:555
  46.6 1.8 %collective-permute-done.11 = f32[40,128]{1,0:T(8,128)S(1)} collective-permute-done((f32[40,128]{1,0:T(8,128)S(1)}, f32[40,128]{1,0:T(8,128)S(1)}, u32[]{:S(2)}, u32[]{:S(2)}) %collective-permute-start.11) | collective-permute-done | bytes 20512 | tf_op jit(solution)/shard_map/ppermute | solution.py:555
  48.4 3.1 %collective-permute-start.12 = (f32[40,128]{1,0:T(8,128)S(1)}, f32[40,128]{1,0:T(8,128)S(1)}, u32[]{:S(2)}, u32[]{:S(2)}) collective-permute-start(f32[40,128]{1,0:T(8,128)S(1)} %add.13), channel_id=1, source_target_pairs={{0,4},{1,5},{2,6},{3,7},{4,0},{5,1},{6,2},{7,3},{8,12},{9,13},{10,... | collective-permute-start | bytes 61448 | tf_op jit(solution)/shard_map/ppermute | solution.py:555
  51.5 1.8 %collective-permute-done.12 = f32[40,128]{1,0:T(8,128)S(1)} collective-permute-done((f32[40,128]{1,0:T(8,128)S(1)}, f32[40,128]{1,0:T(8,128)S(1)}, u32[]{:S(2)}, u32[]{:S(2)}) %collective-permute-start.12) | collective-permute-done | bytes 20512 | tf_op jit(solution)/shard_map/ppermute | solution.py:555
  53.3 0.0 collective-permute-start.13
  53.3 1.2 %collective-permute-done.13 = f32[40,128]{1,0:T(8,128)S(1)} collective-permute-done((f32[40,128]{1,0:T(8,128)S(1)}, f32[40,128]{1,0:T(8,128)S(1)}, u32[]{:S(2)}, u32[]{:S(2)}) %collective-permute-start.13) | collective-permute-done | bytes 20512 | tf_op jit(solution)/shard_map/ppermute | solution.py:555
  54.5 1.5 %collective-permute-start.14 = (f32[40,128]{1,0:T(8,128)S(1)}, f32[40,128]{1,0:T(8,128)S(1)}, u32[]{:S(2)}, u32[]{:S(2)}) collective-permute-start(f32[40,128]{1,0:T(8,128)S(1)} %add.15.one_ref), channel_id=1, source_target_pairs={{0,16},{1,17},{2,18},{3,19},{4,20},{5,21},{6,22},{7,23},{8,24},{9,... | collective-permute-start | bytes 61448 | tf_op jit(solution)/shard_map/ppermute | solution.py:555
  56.0 2.3 %collective-permute-done.14.two_ref = f32[40,128]{1,0:T(8,128)S(1)} collective-permute-done((f32[40,128]{1,0:T(8,128)S(1)}, f32[40,128]{1,0:T(8,128)S(1)}, u32[]{:S(2)}, u32[]{:S(2)}) %collective-permute-start.14) | collective-permute-done | bytes 20512 | tf_op jit(solution)/shard_map/ppermute | solution.py:555
  58.3 0.7 %finish.1 = (f32[1,1]{1,0:T(1,128)}, f32[32,27]{1,0:T(8,128)}, f32[1,32]{1,0:T(1,128)}, f32[32,27]{1,0:T(8,128)}, f32[1,1]{1,0:T(1,128)}) custom-call(f32[40,128]{1,0:T(8,128)S(1)} %add.15.one_ref, f32[40,128]{1,0:T(8,128)S(1)} %collective-permute-done.14.two_ref), custom_call_target="tpu_custom_call" | custom-call | tf_op jit(solution)/shard_map/finish/pallas_call | solution.py:561
  (6 shorter events, 0.0 us)
Async XLA Ops:
  2.7 9.6 %collective-permute-start.4 = (bf16[2,16,1152]{2,1,0:T(8,128)(2,1)S(1)}, bf16[2,16,1152]{2,1,0:T(8,128)(2,1)S(1)}, u32[]{:S(2)}, u32[]{:S(2)}) collective-permute-start(bf16[2,16,1152]{2,1,0:T(8,128)(2,1)S(1)} %get-tuple-element.51), channel_id=1, source_target_pairs={{0,1},{1,0},{2,3},{3,2},{4,5},{5,4},{6,7},{7,6},{8,9},{9,8},{10,11... | collective-permute-start | bytes 221192 | tf_op jit(solution)/shard_map/ppermute | solution.py:586
  5.7 10.2 %collective-permute-start.5 = (bf16[2,16,1152]{2,1,0:T(8,128)(2,1)S(1)}, bf16[2,16,1152]{2,1,0:T(8,128)(2,1)S(1)}, u32[]{:S(2)}, u32[]{:S(2)}) collective-permute-start(bf16[2,16,1152]{2,1,0:T(8,128)(2,1)S(1)} %get-tuple-element.52), channel_id=1, source_target_pairs={{0,2},{1,3},{2,0},{3,1},{4,6},{5,7},{6,4},{7,5},{8,10},{9,11},{10,... | collective-permute-start | bytes 221192 | tf_op jit(solution)/shard_map/ppermute | solution.py:586
  7.3 8.6 %collective-permute-start.6 = (bf16[2,16,1152]{2,1,0:T(8,128)(2,1)S(1)}, bf16[2,16,1152]{2,1,0:T(8,128)(2,1)S(1)}, u32[]{:S(2)}, u32[]{:S(2)}) collective-permute-start(bf16[2,16,1152]{2,1,0:T(8,128)(2,1)S(1)} %get-tuple-element.53), channel_id=1, source_target_pairs={{0,3},{1,2},{2,1},{3,0},{4,7},{5,6},{6,5},{7,4},{8,11},{9,10},{10,... | collective-permute-start | bytes 221192 | tf_op jit(solution)/shard_map/ppermute | solution.py:586
  7.3 14.6 %collective-permute-start = (bf16[2,16,1152]{2,1,0:T(8,128)(2,1)S(1)}, bf16[2,16,1152]{2,1,0:T(8,128)(2,1)S(1)}, u32[]{:S(2)}, u32[]{:S(2)}) collective-permute-start(bf16[2,16,1152]{2,1,0:T(8,128)(2,1)S(1)} %get-tuple-element.46), channel_id=1, source_target_pairs={{0,4},{1,5},{2,6},{3,7},{4,0},{5,1},{6,2},{7,3},{8,12},{9,13},{10,... | collective-permute-start | bytes 221192 | tf_op jit(solution)/shard_map/ppermute | solution.py:586
  10.3 11.6 %collective-permute-start.1 = (bf16[2,16,1152]{2,1,0:T(8,128)(2,1)S(1)}, bf16[2,16,1152]{2,1,0:T(8,128)(2,1)S(1)}, u32[]{:S(2)}, u32[]{:S(2)}) collective-permute-start(bf16[2,16,1152]{2,1,0:T(8,128)(2,1)S(1)} %get-tuple-element.47), channel_id=1, source_target_pairs={{0,5},{1,4},{2,7},{3,6},{4,1},{5,0},{6,3},{7,2},{8,13},{9,12},{10,... | collective-permute-start | bytes 221192 | tf_op jit(solution)/shard_map/ppermute | solution.py:586
  12.2 9.7 %collective-permute-start.2 = (bf16[2,16,1152]{2,1,0:T(8,128)(2,1)S(1)}, bf16[2,16,1152]{2,1,0:T(8,128)(2,1)S(1)}, u32[]{:S(2)}, u32[]{:S(2)}) collective-permute-start(bf16[2,16,1152]{2,1,0:T(8,128)(2,1)S(1)} %get-tuple-element.48), channel_id=1, source_target_pairs={{0,6},{1,7},{2,4},{3,5},{4,2},{5,3},{6,0},{7,1},{8,14},{9,15},{10,... | collective-permute-start | bytes 221192 | tf_op jit(solution)/shard_map/ppermute | solution.py:586
  15.9 7.2 %collective-permute-start.3 = (bf16[2,16,1152]{2,1,0:T(8,128)(2,1)S(1)}, bf16[2,16,1152]{2,1,0:T(8,128)(2,1)S(1)}, u32[]{:S(2)}, u32[]{:S(2)}) collective-permute-start(bf16[2,16,1152]{2,1,0:T(8,128)(2,1)S(1)} %get-tuple-element.49), channel_id=1, source_target_pairs={{0,7},{1,6},{2,5},{3,4},{4,3},{5,2},{6,1},{7,0},{8,15},{9,14},{10,... | collective-permute-start | bytes 221192 | tf_op jit(solution)/shard_map/ppermute | solution.py:586
  15.9 4.8 %copy-start.2 = (f32[32]{0:T(128)S(1)}, f32[32]{0:T(128)}, u32[]{:S(2)}) copy-start(f32[32]{0:T(128)} %param.9) | copy-start | bytes 388
  15.9 4.9 %copy-start = (f32[32,27]{1,0:T(8,128)S(1)}, f32[32,27]{1,0:T(8,128)}, u32[]{:S(2)}) copy-start(f32[32,27]{1,0:T(8,128)} %param.8) | copy-start | bytes 10372
  15.9 4.9 %copy-start.1 = (f32[32,27]{1,0:T(8,128)S(1)}, f32[32,27]{1,0:T(8,128)}, u32[]{:S(2)}) copy-start(f32[32,27]{1,0:T(8,128)} %param.10) | copy-start | bytes 10372
  27.2 1.9 %collective-permute-start.7 = (f32[8,8,1024]{2,1,0:T(8,128)S(1)}, f32[8,8,1024]{2,1,0:T(8,128)S(1)}, u32[]{:S(2)}, u32[]{:S(2)}) collective-permute-start(f32[8,8,1024]{2,1,0:T(8,128)S(1)} %get-tuple-element.68), channel_id=1, source_target_pairs={{0,8},{1,9},{2,10},{3,11},{4,12},{5,13},{6,14},{7,15},{8,0},{9,1},... | collective-permute-start | bytes 786440 | tf_op jit(solution)/shard_map/ppermute | solution.py:586
  27.3 6.7 %collective-permute-start.8 = (f32[4,8,1024]{2,1,0:T(8,128)S(1)}, f32[4,8,1024]{2,1,0:T(8,128)S(1)}, u32[]{:S(2)}, u32[]{:S(2)}) collective-permute-start(f32[4,8,1024]{2,1,0:T(8,128)S(1)} %get-tuple-element.76), channel_id=1, source_target_pairs={{0,16},{1,17},{2,18},{3,19},{4,20},{5,21},{6,22},{7,23},{8,24},{9,... | collective-permute-start | bytes 393224 | tf_op jit(solution)/shard_map/ppermute | solution.py:613
  28.9 6.6 %collective-permute-start.9 = (f32[4,8,1024]{2,1,0:T(8,128)S(1)}, f32[4,8,1024]{2,1,0:T(8,128)S(1)}, u32[]{:S(2)}, u32[]{:S(2)}) collective-permute-start(f32[4,8,1024]{2,1,0:T(8,128)S(1)} %get-tuple-element.77), channel_id=1, source_target_pairs={{0,24},{1,25},{2,26},{3,27},{4,28},{5,29},{6,30},{7,31},{8,16},{9,... | collective-permute-start | bytes 393224 | tf_op jit(solution)/shard_map/ppermute | solution.py:614
  40.5 3.8 %collective-permute-start.10 = (f32[40,128]{1,0:T(8,128)S(1)}, f32[40,128]{1,0:T(8,128)S(1)}, u32[]{:S(2)}, u32[]{:S(2)}) collective-permute-start(f32[40,128]{1,0:T(8,128)S(1)} %get-tuple-element.79), channel_id=1, source_target_pairs={{0,1},{1,0},{2,3},{3,2},{4,5},{5,4},{6,7},{7,6},{8,9},{9,8},{10,11... | collective-permute-start | bytes 61448 | tf_op jit(solution)/shard_map/ppermute | solution.py:555
  44.4 4.0 %collective-permute-start.11 = (f32[40,128]{1,0:T(8,128)S(1)}, f32[40,128]{1,0:T(8,128)S(1)}, u32[]{:S(2)}, u32[]{:S(2)}) collective-permute-start(f32[40,128]{1,0:T(8,128)S(1)} %add.12), channel_id=1, source_target_pairs={{0,2},{1,3},{2,0},{3,1},{4,6},{5,7},{6,4},{7,5},{8,10},{9,11},{10,... | collective-permute-start | bytes 61448 | tf_op jit(solution)/shard_map/ppermute | solution.py:555
  48.4 4.9 %collective-permute-start.12 = (f32[40,128]{1,0:T(8,128)S(1)}, f32[40,128]{1,0:T(8,128)S(1)}, u32[]{:S(2)}, u32[]{:S(2)}) collective-permute-start(f32[40,128]{1,0:T(8,128)S(1)} %add.13), channel_id=1, source_target_pairs={{0,4},{1,5},{2,6},{3,7},{4,0},{5,1},{6,2},{7,3},{8,12},{9,13},{10,... | collective-permute-start | bytes 61448 | tf_op jit(solution)/shard_map/ppermute | solution.py:555
  53.3 1.2 %collective-permute-start.13 = (f32[40,128]{1,0:T(8,128)S(1)}, f32[40,128]{1,0:T(8,128)S(1)}, u32[]{:S(2)}, u32[]{:S(2)}) collective-permute-start(f32[40,128]{1,0:T(8,128)S(1)} %add.14), channel_id=1, source_target_pairs={{0,8},{1,9},{2,10},{3,11},{4,12},{5,13},{6,14},{7,15},{8,0},{9,1},... | collective-permute-start | bytes 61448 | tf_op jit(solution)/shard_map/ppermute | solution.py:555
  54.5 3.8 %collective-permute-start.14 = (f32[40,128]{1,0:T(8,128)S(1)}, f32[40,128]{1,0:T(8,128)S(1)}, u32[]{:S(2)}, u32[]{:S(2)}) collective-permute-start(f32[40,128]{1,0:T(8,128)S(1)} %add.15.one_ref), channel_id=1, source_target_pairs={{0,16},{1,17},{2,18},{3,19},{4,20},{5,21},{6,22},{7,23},{8,24},{9,... | collective-permute-start | bytes 61448 | tf_op jit(solution)/shard_map/ppermute | solution.py:555
where the time goes:
time: 59.1 us; the launch traced here: 58.9 us
  Pallas kernels  22.4 us (38%)
  starting transfers between devices  22 us (37%)
  waiting for transfers between devices  12.9 us (22%)
  between operations  1.41 us (2%)
    ppermute x8, starting transfers between devices, exchange(): lax.ppermute(value, BOTH, [(i, i ^ distance) for i in range(devices)])  12.7 us
    ppermute x5, waiting for transfers between devices, sum_everywhere(): lax.ppermute(value, BOTH, [(i, i ^ apart) for i in range(devices)])  10.2 us
    pallas_call x2, Pallas kernels, project(): pl.pallas_call(functools.partial(project_kernel, count, scale), out_shape...  8.97 us
    ppermute x5, starting transfers between devices, sum_everywhere(): lax.ppermute(value, BOTH, [(i, i ^ apart) for i in range(devices)])  7.48 us
    pallas_call x1, Pallas kernels, backward(): pl.pallas_call(functools.partial(backward_kernel, cells, len(parts) // 2)...  5.02 us
    pallas_call x1, Pallas kernels, forward(): pl.pallas_call(forward_kernel, out_shape=(own, own, jax.ShapeDtypeStruct(...  4.8 us
    pallas_call x1, Pallas kernels, pack(): pl.pallas_call(functools.partial(pack_kernel, depth), out_shape=(jax.Shap...  2.02 us
    ppermute x1, starting transfers between devices, body(): parts.append(lax.ppermute(own, BOTH, straight))  1.55 us
  transfers between devices with their start and end apart: 15, of which 7 were waited for; matrix products, arithmetic and copies ran while one was open for 0% of the time, Pallas kernels for 18%

commit v1 on v0

--- a/solution.py
+++ b/solution.py
@@ -125,8 +125,8 @@
 
 def project_kernel(count, scale, *refs):
     data_refs = refs[:count]
-    init_refs = refs[count:-9]
-    mine_ref, other_ref, own_ref, away_ref, low_ref, high_ref, tab_ref, scal_ref, sem = refs[-9:]
+    init_refs = refs[count:-7]
+    mine_ref, other_ref, low_ref, high_ref, tab_ref, scal_ref, sem = refs[-7:]
     each = data_refs[0].shape[0]
     views, rows = count * each, data_refs[0].shape[1]
     window = rows // 2
@@ -222,10 +222,7 @@
             sums = lax.fori_loop(0, views, one_view, sums, unroll=views if distinct else 1)
             for z in range(rows):
                 done = sums[z] * scale if scale else sums[z]
-                at_z = z % window
-                (mine_ref, other_ref)[z // window][at_z, :, cols] = done
-                if scale and HALO <= at_z < window - HALO:
-                    (own_ref, away_ref)[z // window][at_z - HALO, :, cols] = done
+                (mine_ref, other_ref)[z // window][z % window, :, cols] = done
             return carry
 
         lax.fori_loop(0, X // LANES, one_block, 0)
@@ -238,12 +235,11 @@
     count = len(chunks)
     views, rows = count * chunks[0].shape[0], chunks[0].shape[1]
     whole = jax.ShapeDtypeStruct((rows // 2, Y, X), F32)
-    inner = jax.ShapeDtypeStruct((rows // 2 - 2 * HALO if scale else 1, Y, X), F32)
     return pl.pallas_call(
         functools.partial(project_kernel, count, scale),
-        out_shape=(whole, whole, inner, inner),
+        out_shape=(whole, whole),
         in_specs=[VMEM] * (count + len(init)),
-        out_specs=(VMEM,) * 4,
+        out_specs=(VMEM, VMEM),
         scratch_shapes=[
             pltpu.VMEM((views, DW // LANES, rows, LANES), F32),
             pltpu.VMEM((views, DW // LANES, rows, LANES), F32),
@@ -382,23 +378,35 @@
     )(params)
 
 
+def join_kernel(mine_ref, came_ref, own_ref, shifted_ref):
+    rows = mine_ref.shape[0]
+    both = mine_ref[...] + came_ref[...]
+    own_ref[...] = both[HALO : rows - HALO]
+    fill_shifted(shifted_ref, both.reshape(rows * Y, X))
+
+
+def join(mine, came):
+    rows = mine.shape[0]
+    return pl.pallas_call(
+        join_kernel,
+        out_shape=(
+            jax.ShapeDtypeStruct((rows - 2 * HALO, Y, X), F32),
+            jax.ShapeDtypeStruct((3, rows * Y, X), F32),
+        ),
+        in_specs=[VMEM] * 2,
+        out_specs=(VMEM,) * 2,
+        compiler_params=vmem_mib(8),
+        name="join",
+    )(mine, came)
+
+
 def forward_kernel(
-    mine_ref,
-    came_ref,
-    params_ref,
-    first_ref,
-    turned_ref,
-    pred_ref,
-    again_ref,
-    shifted_ref,
-    hidden_ref,
-    acc_ref,
+    shifted_ref, params_ref, first_ref, turned_ref, pred_ref, again_ref, hidden_ref, acc_ref
 ):
-    rows = mine_ref.shape[0]
+    rows = shifted_ref.shape[1] // Y
     hidden_count = rows - 2
     height = first_ref.shape[0]
     first = first_ref[...]
-    fill_shifted(shifted_ref, (mine_ref[...] + came_ref[...]).reshape(rows * Y, X))
     acc_ref[...] = jnp.zeros(acc_ref.shape, F32)
 
     def one_slice(hidden_slice, carry):
@@ -429,8 +437,8 @@
     again_ref[...] = pred
 
 
-def forward(mine, came, params, first, turned):
-    rows = mine.shape[0]
+def forward(shifted, params, first, turned):
+    rows = shifted.shape[1] // Y
     height = first.shape[0]
     own = jax.ShapeDtypeStruct((rows - 2 * HALO, Y, X), F32)
     return pl.pallas_call(
@@ -438,18 +446,17 @@
         out_shape=(
             own,
             own,
-            jax.ShapeDtypeStruct((3, rows * Y, X), F32),
             jax.ShapeDtypeStruct(((rows - 2) * height, X), BF16),
         ),
-        in_specs=[VMEM] * 5,
-        out_specs=(VMEM,) * 4,
+        in_specs=[VMEM] * 4,
+        out_specs=(VMEM,) * 3,
         scratch_shapes=[pltpu.VMEM((3, rows * Y, X), F32)],
         cost_estimate=pl.CostEstimate(
             flops=20_000_000_000, bytes_accessed=2_000_000, transcendentals=0
         ),
         compiler_params=vmem_mib(18),
         name="forward",
-    )(mine, came, params, first, turned)
+    )(shifted, params, first, turned)
 
 
 def padded_rows(high, low):
@@ -458,8 +465,8 @@
 
 
 def backward_kernel(cells, others, shifted_ref, hidden_ref, pred_ref, second_ref, *refs):
-    part_refs = refs[: 2 * others]
-    out_ref, target_out_ref, grad_ref, acc1_ref, acc2_ref = refs[2 * others :]
+    part_refs = refs[:others]
+    out_ref, target_out_ref, grad_ref, acc1_ref, acc2_ref = refs[others:]
     rows = shifted_ref.shape[1] // Y
     hidden_count = rows - 2
     height = second_ref.shape[0]
@@ -520,7 +527,7 @@
 def backward(shifted, hidden, pred, parts, second, cells):
     height = second.shape[0]
     return pl.pallas_call(
-        functools.partial(backward_kernel, cells, len(parts) // 2),
+        functools.partial(backward_kernel, cells, len(parts)),
         out_shape=(
             jax.ShapeDtypeStruct((height // Y + 8, LANES), F32),
             jax.ShapeDtypeStruct(pred.shape, F32),
@@ -588,7 +595,7 @@
     arrived = [sent[0]] + [None] * (n_slab - 1)
     for distance in range(1, n_slab):
         arrived[distance] = exchange(sent[distance], distance)
-    near = n_slab // 2
+    near = n_slab // 2 + 1
     sums = project(arrived[:near], (), 0.0)
     sums, w_first, b_first, w_second, b_second = lax.optimization_barrier(
         (sums, w_first, b_first, w_second, b_second)
@@ -604,16 +611,15 @@
         axis=1,
     )
     sums, (first, second, turned) = lax.optimization_barrier((sums, weights(params)))
-    mine, other, own, away = project(arrived[near:], sums[:2], scale)
+    mine, other = project(arrived[near:], sums, scale)
     came = exchange(other, n_slab)
+    own, shifted = join(mine, came)
     parts = []
     for apart in range(1, n_sub):
-        straight = [(i, (i + apart * group) % devices) for i in range(devices)]
-        crossed = [(i, j ^ n_slab) for i, j in straight]
-        parts.append(lax.ppermute(own, BOTH, straight))
-        parts.append(lax.ppermute(away, BOTH, crossed))
-
-    pred, again, shifted, hidden = forward(mine, came, params, first, turned)
+        pairs = [(i, (i + apart * group) % devices) for i in range(devices)]
+        parts.append(lax.ppermute(own, BOTH, pairs))
+
+    pred, again, hidden = forward(shifted, params, first, turned)
     partial, target = backward(shifted, hidden, again, parts, second, cells)
     loss, grad_w1, grad_b1, grad_w2, grad_b2 = sum_everywhere(partial, channels)
     return (

time: 59.1 us -> 58.5 us (0.990)
    ppermute x2 -> x1, waiting for transfers between devices: 1.51 us -> 0.01 us  [body(): parts.append(lax.ppermute(own, BOTH, pairs))]
    ppermute x8, waiting for transfers between devices: 1.15 us -> 2.6 us  [exchange(): lax.ppermute(value, BOTH, [(i, i ^ distance) for i in range(devices)])]
    pallas_call x2, Pallas kernels: 8.97 us -> 8.35 us  [project(): pl.pallas_call(functools.partial(project_kernel, count, scale), out_shape...]
    ppermute x2 -> x1, starting transfers between devices: 1.85 us -> 1.56 us  [body(): parts.append(lax.ppermute(own, BOTH, pairs))]
    pallas_call x1 -> x2, Pallas kernels: 5.02 us -> 5.26 us  [the longest x1 5.05 us: backward(): pl.pallas_call(functools.partial(backward_kernel, cells, len(parts)), out...]
  transfers between devices with their start and end apart: 15 -> 14, of which waited for: 7 -> 7; matrix products, arithmetic and copies ran while one was open for 0% -> 0% of each run, Pallas kernels for 18% -> 18%
where the time goes in v1:
time: 58.5 us; the launch traced here: 58.3 us
  starting transfers between devices  22.2 us (38%)
  Pallas kernels  21.9 us (37%)
  waiting for transfers between devices  12.6 us (22%)
  between operations  1.42 us (2%)
    ppermute x8, starting transfers between devices, exchange(): lax.ppermute(value, BOTH, [(i, i ^ distance) for i in range(devices)])  12.7 us
    ppermute x5, waiting for transfers between devices, sum_everywhere(): lax.ppermute(value, BOTH, [(i, i ^ apart) for i in range(devices)])  10 us
    pallas_call x2, Pallas kernels, project(): pl.pallas_call(functools.partial(project_kernel, count, scale), out_shape...  8.35 us
    ppermute x5, starting transfers between devices, sum_everywhere(): lax.ppermute(value, BOTH, [(i, i ^ apart) for i in range(devices)])  7.97 us
    pallas_call x1, Pallas kernels, backward(): pl.pallas_call(functools.partial(backward_kernel, cells, len(parts)), out...  5.05 us
    pallas_call x1, Pallas kernels, forward(): pl.pallas_call(forward_kernel, out_shape=(own, own, jax.ShapeDtypeStruct(...  4.61 us
    ppermute x8, waiting for transfers between devices, exchange(): lax.ppermute(value, BOTH, [(i, i ^ distance) for i in range(devices)])  2.6 us
    pallas_call x1, Pallas kernels, pack(): pl.pallas_call(functools.partial(pack_kernel, depth), out_shape=(jax.Shap...  2.02 us
  transfers between devices with their start and end apart: 14, of which 7 were waited for; matrix products, arithmetic and copies ran while one was open for 0% of the time, Pallas kernels for 18%

profile of v1, /device:TPU:0, one launch (start us, length us, event | category | flops | bytes accessed | tf_op | source)
XLA Modules:
  0.0 58.3 jit_solution(15703779061289469718)
XLA Ops:
  0.6 2.0 %pack.1 = (bf16[2,16,1152]{2,1,0:T(8,128)(2,1)S(1)}, bf16[2,16,1152]{2,1,0:T(8,128)(2,1)S(1)}, bf16[2,16,1152]{2,1,0:T(8,128)(2,1)S(1)}, bf16[2,16,1152]{2,1,0:T...) custom-call(f32[2]{0:T(128)} %angle_ref.1, ...), custom_call_target="tpu_custom_call" | custom-call | tf_op jit(solution)/shard_map/pack/pallas_call | solution.py:107
  2.7 3.1 %collective-permute-start.3 = (bf16[2,16,1152]{2,1,0:T(8,128)(2,1)S(1)}, bf16[2,16,1152]{2,1,0:T(8,128)(2,1)S(1)}, u32[]{:S(2)}, u32[]{:S(2)}) collective-permute-start(bf16[2,16,1152]{2,1,0:T(8,128)(2,1)S(1)} %get-tuple-element.49), channel_id=1, source_target_pairs={{0,1},{1,0},{2,3},{3,2},{4,5},{5,4},{6,7},{7,6},{8,9},{9,8},{10,11... | collective-permute-start | bytes 221192 | tf_op jit(solution)/shard_map/ppermute | solution.py:593
  5.7 1.6 %collective-permute-start.4 = (bf16[2,16,1152]{2,1,0:T(8,128)(2,1)S(1)}, bf16[2,16,1152]{2,1,0:T(8,128)(2,1)S(1)}, u32[]{:S(2)}, u32[]{:S(2)}) collective-permute-start(bf16[2,16,1152]{2,1,0:T(8,128)(2,1)S(1)} %get-tuple-element.50), channel_id=1, source_target_pairs={{0,2},{1,3},{2,0},{3,1},{4,6},{5,7},{6,4},{7,5},{8,10},{9,11},{10,... | collective-permute-start | bytes 221192 | tf_op jit(solution)/shard_map/ppermute | solution.py:593
  7.3 0.0 collective-permute-start.5
  7.3 3.0 %collective-permute-start.6 = (bf16[2,16,1152]{2,1,0:T(8,128)(2,1)S(1)}, bf16[2,16,1152]{2,1,0:T(8,128)(2,1)S(1)}, u32[]{:S(2)}, u32[]{:S(2)}) collective-permute-start(bf16[2,16,1152]{2,1,0:T(8,128)(2,1)S(1)} %get-tuple-element.52), channel_id=1, source_target_pairs={{0,4},{1,5},{2,6},{3,7},{4,0},{5,1},{6,2},{7,3},{8,12},{9,13},{10,... | collective-permute-start | bytes 221192 | tf_op jit(solution)/shard_map/ppermute | solution.py:593
  10.3 1.3 %collective-permute-start = (bf16[2,16,1152]{2,1,0:T(8,128)(2,1)S(1)}, bf16[2,16,1152]{2,1,0:T(8,128)(2,1)S(1)}, u32[]{:S(2)}, u32[]{:S(2)}) collective-permute-start(bf16[2,16,1152]{2,1,0:T(8,128)(2,1)S(1)} %get-tuple-element.45), channel_id=1, source_target_pairs={{0,5},{1,4},{2,7},{3,6},{4,1},{5,0},{6,3},{7,2},{8,13},{9,12},{10,... | collective-permute-start | bytes 221192 | tf_op jit(solution)/shard_map/ppermute | solution.py:593
  12.2 0.0 collective-permute-done.3.refs_1_
  12.2 3.7 %collective-permute-start.1 = (bf16[2,16,1152]{2,1,0:T(8,128)(2,1)S(1)}, bf16[2,16,1152]{2,1,0:T(8,128)(2,1)S(1)}, u32[]{:S(2)}, u32[]{:S(2)}) collective-permute-start(bf16[2,16,1152]{2,1,0:T(8,128)(2,1)S(1)} %get-tuple-element.46), channel_id=1, source_target_pairs={{0,6},{1,7},{2,4},{3,5},{4,2},{5,3},{6,0},{7,1},{8,14},{9,15},{10,... | collective-permute-start | bytes 221192 | tf_op jit(solution)/shard_map/ppermute | solution.py:593
  15.9 0.0 collective-permute-done.4.refs_2_
  15.9 0.0 collective-permute-start.2
  15.9 0.0 collective-permute-done.5.refs_3_
  15.9 0.0 collective-permute-done.6.refs_4_
  15.9 0.0 copy-start.2
  15.9 0.0 copy-start
  16.0 0.0 copy-start.1
  16.0 4.9 %project.2 = (f32[8,8,1024]{2,1,0:T(8,128)S(1)}, f32[8,8,1024]{2,1,0:T(8,128)S(1)}) custom-call(bf16[2,16,1152]{2,1,0:T(8,128)(2,1)S(1)} %get-tuple-element.48.refs_0_, bf16[2,16,1152]{2,1,0:T(8,128)(2,1)S(1)} %collective-permute-done.3.refs_1_, bf16[2,16,1152]{2,1,0:T(8,128)(2,1)S(1)} %collective-permute-done.4.refs_2_, ...), custom_call_target="tpu_custom_call" | custom-call | flops 4000000000 | bytes 1500000 | tf_op jit(solution)/shard_map/project/pallas_call | solution.py:238
  20.8 0.0 copy-done.2
  20.8 0.1 copy.13
  20.9 0.0 copy-done
  20.9 0.0 copy-done.1
  21.0 0.1 concatenate.3.params_ref
  21.0 0.9 %weights.1 = (bf16[256,256]{1,0:T(8,128)(2,1)S(1)}, bf16[256,256]{1,0:T(8,128)(2,1)S(1)}, bf16[256,256]{1,0:T(8,128)(2,1)S(1)}) custom-call(f32[32,128]{1,0:T(8,128)S(1)} %concatenate.3.params_ref), custom_call_target="tpu_custom_call" | custom-call | tf_op jit(solution)/shard_map/weights/pallas_call | solution.py:367
  22.0 0.0 collective-permute-done.refs_0_
  22.0 0.0 collective-permute-done.1.refs_1_
  22.0 1.1 %collective-permute-done.2.refs_2_ = bf16[2,16,1152]{2,1,0:T(8,128)(2,1)S(1)} collective-permute-done((bf16[2,16,1152]{2,1,0:T(8,128)(2,1)S(1)}, bf16[2,16,1152]{2,1,0:T(8,128)(2,1)S(1)}, u32[]{:S(2)}, u32[]{:S(2)}) %collective-permute-start.2) | collective-permute-done | bytes 73760 | tf_op jit(solution)/shard_map/ppermute | solution.py:593
  23.1 3.5 %project.3 = (f32[8,8,1024]{2,1,0:T(8,128)S(1)}, f32[8,8,1024]{2,1,0:T(8,128)S(1)}) custom-call(bf16[2,16,1152]{2,1,0:T(8,128)(2,1)S(1)} %collective-permute-done.refs_0_, bf16[2,16,1152]{2,1,0:T(8,128)(2,1)S(1)} %collective-permute-done.1.refs_1_, bf16[2,16,1152]{2,1,0:T(8,128)(2,1)S(1)} %collective-permute-done.2.refs_2_, ...), custom_call_target="tpu_custom_call" | custom-call | flops 4000000000 | bytes 1500000 | tf_op jit(solution)/shard_map/project/pallas_call | solution.py:238
  26.6 0.1 collective-permute-start.7
  26.6 1.5 %collective-permute-done.7.came_ref = f32[8,8,1024]{2,1,0:T(8,128)S(1)} collective-permute-done((f32[8,8,1024]{2,1,0:T(8,128)S(1)}, f32[8,8,1024]{2,1,0:T(8,128)S(1)}, u32[]{:S(2)}, u32[]{:S(2)}) %collective-permute-start.7) | collective-permute-done | bytes 262176 | tf_op jit(solution)/shard_map/ppermute | solution.py:593
  28.2 0.2 join.1
  28.4 1.6 %collective-permute-start.8 = (f32[4,8,1024]{2,1,0:T(8,128)S(1)}, f32[4,8,1024]{2,1,0:T(8,128)S(1)}, u32[]{:S(2)}, u32[]{:S(2)}) collective-permute-start(f32[4,8,1024]{2,1,0:T(8,128)S(1)} %get-tuple-element.75), channel_id=1, source_target_pairs={{0,16},{1,17},{2,18},{3,19},{4,20},{5,21},{6,22},{7,23},{8,24},{9,... | collective-permute-start | bytes 393224 | tf_op jit(solution)/shard_map/ppermute | solution.py:620
  29.9 4.6 %forward.1 = (f32[4,8,1024]{2,1,0:T(8,128)}, f32[4,8,1024]{2,1,0:T(8,128)S(1)}, bf16[1536,1024]{1,0:T(8,128)(2,1)S(1)}) custom-call(f32[3,64,1024]{2,1,0:T(8,128)S(1)} %get-tuple-element.68.shifted_ref, f32[32,128]{1,0:T(8,128)S(1)} %concatenate.3.params_ref, bf16[256,256]{1,0:T(8,128)(2,1)S(1)} %get-tuple-element.69.first_ref, ...), custom_call_target="tpu_custom_call" | custom-call | flops 20000000000 | bytes 2000000 | tf_op jit(solution)/shard_map/forward/pallas_call | solution.py:444
  34.6 0.0 collective-permute-done.8.refs_0_
  34.6 5.1 %backward.1 = (f32[40,128]{1,0:T(8,128)S(1)}, f32[4,8,1024]{2,1,0:T(8,128)}) custom-call(f32[3,64,1024]{2,1,0:T(8,128)S(1)} %get-tuple-element.68.shifted_ref, bf16[1536,1024]{1,0:T(8,128)(2,1)S(1)} %get-tuple-element.72.hidden_ref, f32[4,8,1024]{2,1,0:T(8,128)S(1)} %get-tuple-element.73.pred_ref, bf16[256,256]{1,0:T(8,128)(2,1)S(1)} %get-tuple-element.74.second_ref, ...), custom_call_target="tpu_custom_call" | custom-call | tf_op jit(solution)/shard_map/backward/pallas_call | solution.py:529
  39.6 2.8 %collective-permute-start.9 = (f32[40,128]{1,0:T(8,128)S(1)}, f32[40,128]{1,0:T(8,128)S(1)}, u32[]{:S(2)}, u32[]{:S(2)}) collective-permute-start(f32[40,128]{1,0:T(8,128)S(1)} %get-tuple-element.77), channel_id=1, source_target_pairs={{0,1},{1,0},{2,3},{3,2},{4,5},{5,4},{6,7},{7,6},{8,9},{9,8},{10,11... | collective-permute-start | bytes 61448 | tf_op jit(solution)/shard_map/ppermute | solution.py:562
  42.4 1.8 %collective-permute-done.9 = f32[40,128]{1,0:T(8,128)S(1)} collective-permute-done((f32[40,128]{1,0:T(8,128)S(1)}, f32[40,128]{1,0:T(8,128)S(1)}, u32[]{:S(2)}, u32[]{:S(2)}) %collective-permute-start.9) | collective-permute-done | bytes 20512 | tf_op jit(solution)/shard_map/ppermute | solution.py:562
  44.2 1.5 %collective-permute-start.10 = (f32[40,128]{1,0:T(8,128)S(1)}, f32[40,128]{1,0:T(8,128)S(1)}, u32[]{:S(2)}, u32[]{:S(2)}) collective-permute-start(f32[40,128]{1,0:T(8,128)S(1)} %add.12), channel_id=1, source_target_pairs={{0,2},{1,3},{2,0},{3,1},{4,6},{5,7},{6,4},{7,5},{8,10},{9,11},{10,... | collective-permute-start | bytes 61448 | tf_op jit(solution)/shard_map/ppermute | solution.py:562
  45.7 2.2 %collective-permute-done.10 = f32[40,128]{1,0:T(8,128)S(1)} collective-permute-done((f32[40,128]{1,0:T(8,128)S(1)}, f32[40,128]{1,0:T(8,128)S(1)}, u32[]{:S(2)}, u32[]{:S(2)}) %collective-permute-start.10) | collective-permute-done | bytes 20512 | tf_op jit(solution)/shard_map/ppermute | solution.py:562
  48.0 2.7 %collective-permute-start.11 = (f32[40,128]{1,0:T(8,128)S(1)}, f32[40,128]{1,0:T(8,128)S(1)}, u32[]{:S(2)}, u32[]{:S(2)}) collective-permute-start(f32[40,128]{1,0:T(8,128)S(1)} %add.13), channel_id=1, source_target_pairs={{0,4},{1,5},{2,6},{3,7},{4,0},{5,1},{6,2},{7,3},{8,12},{9,13},{10,... | collective-permute-start | bytes 61448 | tf_op jit(solution)/shard_map/ppermute | solution.py:562
  50.7 2.0 %collective-permute-done.11 = f32[40,128]{1,0:T(8,128)S(1)} collective-permute-done((f32[40,128]{1,0:T(8,128)S(1)}, f32[40,128]{1,0:T(8,128)S(1)}, u32[]{:S(2)}, u32[]{:S(2)}) %collective-permute-start.11) | collective-permute-done | bytes 20512 | tf_op jit(solution)/shard_map/ppermute | solution.py:562
  52.6 0.0 collective-permute-start.12
  52.6 1.2 %collective-permute-done.12 = f32[40,128]{1,0:T(8,128)S(1)} collective-permute-done((f32[40,128]{1,0:T(8,128)S(1)}, f32[40,128]{1,0:T(8,128)S(1)}, u32[]{:S(2)}, u32[]{:S(2)}) %collective-permute-start.12) | collective-permute-done | bytes 20512 | tf_op jit(solution)/shard_map/ppermute | solution.py:562
  53.8 0.9 %collective-permute-start.13 = (f32[40,128]{1,0:T(8,128)S(1)}, f32[40,128]{1,0:T(8,128)S(1)}, u32[]{:S(2)}, u32[]{:S(2)}) collective-permute-start(f32[40,128]{1,0:T(8,128)S(1)} %add.15.one_ref), channel_id=1, source_target_pairs={{0,16},{1,17},{2,18},{3,19},{4,20},{5,21},{6,22},{7,23},{8,24},{9,... | collective-permute-start | bytes 61448 | tf_op jit(solution)/shard_map/ppermute | solution.py:562
  54.8 2.9 %collective-permute-done.13.two_ref = f32[40,128]{1,0:T(8,128)S(1)} collective-permute-done((f32[40,128]{1,0:T(8,128)S(1)}, f32[40,128]{1,0:T(8,128)S(1)}, u32[]{:S(2)}, u32[]{:S(2)}) %collective-permute-start.13) | collective-permute-done | bytes 20512 | tf_op jit(solution)/shard_map/ppermute | solution.py:562
  57.6 0.7 %finish.1 = (f32[1,1]{1,0:T(1,128)}, f32[32,27]{1,0:T(8,128)}, f32[1,32]{1,0:T(1,128)}, f32[32,27]{1,0:T(8,128)}, f32[1,1]{1,0:T(1,128)}) custom-call(f32[40,128]{1,0:T(8,128)S(1)} %add.15.one_ref, f32[40,128]{1,0:T(8,128)S(1)} %collective-permute-done.13.two_ref), custom_call_target="tpu_custom_call" | custom-call | tf_op jit(solution)/shard_map/finish/pallas_call | solution.py:568
  (6 shorter events, 0.0 us)
Async XLA Ops:
  2.7 9.6 %collective-permute-start.3 = (bf16[2,16,1152]{2,1,0:T(8,128)(2,1)S(1)}, bf16[2,16,1152]{2,1,0:T(8,128)(2,1)S(1)}, u32[]{:S(2)}, u32[]{:S(2)}) collective-permute-start(bf16[2,16,1152]{2,1,0:T(8,128)(2,1)S(1)} %get-tuple-element.49), channel_id=1, source_target_pairs={{0,1},{1,0},{2,3},{3,2},{4,5},{5,4},{6,7},{7,6},{8,9},{9,8},{10,11... | collective-permute-start | bytes 221192 | tf_op jit(solution)/shard_map/ppermute | solution.py:593
  5.7 10.2 %collective-permute-start.4 = (bf16[2,16,1152]{2,1,0:T(8,128)(2,1)S(1)}, bf16[2,16,1152]{2,1,0:T(8,128)(2,1)S(1)}, u32[]{:S(2)}, u32[]{:S(2)}) collective-permute-start(bf16[2,16,1152]{2,1,0:T(8,128)(2,1)S(1)} %get-tuple-element.50), channel_id=1, source_target_pairs={{0,2},{1,3},{2,0},{3,1},{4,6},{5,7},{6,4},{7,5},{8,10},{9,11},{10,... | collective-permute-start | bytes 221192 | tf_op jit(solution)/shard_map/ppermute | solution.py:593
  7.3 8.6 %collective-permute-start.5 = (bf16[2,16,1152]{2,1,0:T(8,128)(2,1)S(1)}, bf16[2,16,1152]{2,1,0:T(8,128)(2,1)S(1)}, u32[]{:S(2)}, u32[]{:S(2)}) collective-permute-start(bf16[2,16,1152]{2,1,0:T(8,128)(2,1)S(1)} %get-tuple-element.51), channel_id=1, source_target_pairs={{0,3},{1,2},{2,1},{3,0},{4,7},{5,6},{6,5},{7,4},{8,11},{9,10},{10,... | collective-permute-start | bytes 221192 | tf_op jit(solution)/shard_map/ppermute | solution.py:593
  7.3 8.6 %collective-permute-start.6 = (bf16[2,16,1152]{2,1,0:T(8,128)(2,1)S(1)}, bf16[2,16,1152]{2,1,0:T(8,128)(2,1)S(1)}, u32[]{:S(2)}, u32[]{:S(2)}) collective-permute-start(bf16[2,16,1152]{2,1,0:T(8,128)(2,1)S(1)} %get-tuple-element.52), channel_id=1, source_target_pairs={{0,4},{1,5},{2,6},{3,7},{4,0},{5,1},{6,2},{7,3},{8,12},{9,13},{10,... | collective-permute-start | bytes 221192 | tf_op jit(solution)/shard_map/ppermute | solution.py:593
  10.3 11.7 %collective-permute-start = (bf16[2,16,1152]{2,1,0:T(8,128)(2,1)S(1)}, bf16[2,16,1152]{2,1,0:T(8,128)(2,1)S(1)}, u32[]{:S(2)}, u32[]{:S(2)}) collective-permute-start(bf16[2,16,1152]{2,1,0:T(8,128)(2,1)S(1)} %get-tuple-element.45), channel_id=1, source_target_pairs={{0,5},{1,4},{2,7},{3,6},{4,1},{5,0},{6,3},{7,2},{8,13},{9,12},{10,... | collective-permute-start | bytes 221192 | tf_op jit(solution)/shard_map/ppermute | solution.py:593
  12.2 9.8 %collective-permute-start.1 = (bf16[2,16,1152]{2,1,0:T(8,128)(2,1)S(1)}, bf16[2,16,1152]{2,1,0:T(8,128)(2,1)S(1)}, u32[]{:S(2)}, u32[]{:S(2)}) collective-permute-start(bf16[2,16,1152]{2,1,0:T(8,128)(2,1)S(1)} %get-tuple-element.46), channel_id=1, source_target_pairs={{0,6},{1,7},{2,4},{3,5},{4,2},{5,3},{6,0},{7,1},{8,14},{9,15},{10,... | collective-permute-start | bytes 221192 | tf_op jit(solution)/shard_map/ppermute | solution.py:593
  15.9 7.2 %collective-permute-start.2 = (bf16[2,16,1152]{2,1,0:T(8,128)(2,1)S(1)}, bf16[2,16,1152]{2,1,0:T(8,128)(2,1)S(1)}, u32[]{:S(2)}, u32[]{:S(2)}) collective-permute-start(bf16[2,16,1152]{2,1,0:T(8,128)(2,1)S(1)} %get-tuple-element.47), channel_id=1, source_target_pairs={{0,7},{1,6},{2,5},{3,4},{4,3},{5,2},{6,1},{7,0},{8,15},{9,14},{10,... | collective-permute-start | bytes 221192 | tf_op jit(solution)/shard_map/ppermute | solution.py:593
  15.9 4.9 %copy-start.2 = (f32[32]{0:T(128)S(1)}, f32[32]{0:T(128)}, u32[]{:S(2)}) copy-start(f32[32]{0:T(128)} %param.9) | copy-start | bytes 388
  15.9 5.0 %copy-start = (f32[32,27]{1,0:T(8,128)S(1)}, f32[32,27]{1,0:T(8,128)}, u32[]{:S(2)}) copy-start(f32[32,27]{1,0:T(8,128)} %param.8) | copy-start | bytes 10372
  16.0 5.0 %copy-start.1 = (f32[32,27]{1,0:T(8,128)S(1)}, f32[32,27]{1,0:T(8,128)}, u32[]{:S(2)}) copy-start(f32[32,27]{1,0:T(8,128)} %param.10) | copy-start | bytes 10372
  26.6 1.6 %collective-permute-start.7 = (f32[8,8,1024]{2,1,0:T(8,128)S(1)}, f32[8,8,1024]{2,1,0:T(8,128)S(1)}, u32[]{:S(2)}, u32[]{:S(2)}) collective-permute-start(f32[8,8,1024]{2,1,0:T(8,128)S(1)} %get-tuple-element.67), channel_id=1, source_target_pairs={{0,8},{1,9},{2,10},{3,11},{4,12},{5,13},{6,14},{7,15},{8,0},{9,1},... | collective-permute-start | bytes 786440 | tf_op jit(solution)/shard_map/ppermute | solution.py:593
  28.4 6.2 %collective-permute-start.8 = (f32[4,8,1024]{2,1,0:T(8,128)S(1)}, f32[4,8,1024]{2,1,0:T(8,128)S(1)}, u32[]{:S(2)}, u32[]{:S(2)}) collective-permute-start(f32[4,8,1024]{2,1,0:T(8,128)S(1)} %get-tuple-element.75), channel_id=1, source_target_pairs={{0,16},{1,17},{2,18},{3,19},{4,20},{5,21},{6,22},{7,23},{8,24},{9,... | collective-permute-start | bytes 393224 | tf_op jit(solution)/shard_map/ppermute | solution.py:620
  39.6 4.5 %collective-permute-start.9 = (f32[40,128]{1,0:T(8,128)S(1)}, f32[40,128]{1,0:T(8,128)S(1)}, u32[]{:S(2)}, u32[]{:S(2)}) collective-permute-start(f32[40,128]{1,0:T(8,128)S(1)} %get-tuple-element.77), channel_id=1, source_target_pairs={{0,1},{1,0},{2,3},{3,2},{4,5},{5,4},{6,7},{7,6},{8,9},{9,8},{10,11... | collective-permute-start | bytes 61448 | tf_op jit(solution)/shard_map/ppermute | solution.py:562
  44.2 3.8 %collective-permute-start.10 = (f32[40,128]{1,0:T(8,128)S(1)}, f32[40,128]{1,0:T(8,128)S(1)}, u32[]{:S(2)}, u32[]{:S(2)}) collective-permute-start(f32[40,128]{1,0:T(8,128)S(1)} %add.12), channel_id=1, source_target_pairs={{0,2},{1,3},{2,0},{3,1},{4,6},{5,7},{6,4},{7,5},{8,10},{9,11},{10,... | collective-permute-start | bytes 61448 | tf_op jit(solution)/shard_map/ppermute | solution.py:562
  48.0 4.7 %collective-permute-start.11 = (f32[40,128]{1,0:T(8,128)S(1)}, f32[40,128]{1,0:T(8,128)S(1)}, u32[]{:S(2)}, u32[]{:S(2)}) collective-permute-start(f32[40,128]{1,0:T(8,128)S(1)} %add.13), channel_id=1, source_target_pairs={{0,4},{1,5},{2,6},{3,7},{4,0},{5,1},{6,2},{7,3},{8,12},{9,13},{10,... | collective-permute-start | bytes 61448 | tf_op jit(solution)/shard_map/ppermute | solution.py:562
  52.6 1.2 %collective-permute-start.12 = (f32[40,128]{1,0:T(8,128)S(1)}, f32[40,128]{1,0:T(8,128)S(1)}, u32[]{:S(2)}, u32[]{:S(2)}) collective-permute-start(f32[40,128]{1,0:T(8,128)S(1)} %add.14), channel_id=1, source_target_pairs={{0,8},{1,9},{2,10},{3,11},{4,12},{5,13},{6,14},{7,15},{8,0},{9,1},... | collective-permute-start | bytes 61448 | tf_op jit(solution)/shard_map/ppermute | solution.py:562
  53.8 3.8 %collective-permute-start.13 = (f32[40,128]{1,0:T(8,128)S(1)}, f32[40,128]{1,0:T(8,128)S(1)}, u32[]{:S(2)}, u32[]{:S(2)}) collective-permute-start(f32[40,128]{1,0:T(8,128)S(1)} %add.15.one_ref), channel_id=1, source_target_pairs={{0,16},{1,17},{2,18},{3,19},{4,20},{5,21},{6,22},{7,23},{8,24},{9,... | collective-permute-start | bytes 61448 | tf_op jit(solution)/shard_map/ppermute | solution.py:562
